TPU v7x, 256 devices: a whole 4x4x8 slice. The times are simulated.
256 devices in a mesh: rcv: 32 (over z, y), hd: 8 (over x, core).
Axes of the slice: x: 4, y: 4, z: 8, core: 2. Of those that a mesh axis runs over, the one named last changes fastest.
Arguments:
- stream: bfloat16 [32768, 1024], P(('rcv', 'hd')), may hold values from -3 to 3
- queries: bfloat16 [32768, 1024], P(('rcv', 'hd')), may hold values from -9 to 9
- keys: bfloat16 [32768, 1024], P(('rcv', 'hd')), may hold values from -9 to 9
- values: bfloat16 [32768, 1024], P(('rcv', 'hd')), may hold values from -6 to 6
- out_proj: bfloat16 [1024, 1024], replicated, may hold values from -0.375 to 0.375
- norm_gain: float32 [1024], replicated, may hold values from 0.5 to 1.5
- expert_weights: bfloat16 [1024, 64, 3, 512], P(None, 'rcv'), may hold values from -0.1875 to 0.1875
- expert_ids: int32 [32768, 4], P(('rcv', 'hd')), may hold values from 0 to 63, as said below
- gate_weights: float32 [32768, 4], P(('rcv', 'hd')), may hold values from 0.1 to 1
- out_cotangent: bfloat16 [32768, 1024], P(('rcv', 'hd')), may hold values from -6 to 6
Outputs:
- block_out: bfloat16 [32768, 1024], P(('rcv', 'hd'))
- stream_grad: bfloat16 [32768, 1024], P(('rcv', 'hd'))
Inputs may be any that keep to these rules, and one draw needn't show every extreme that they name: `expert_ids`: each token names 4 different experts; its k-th id lies in k * 16 to (k + 1) * 16 - 1. Within each aligned block of 128 rows no expert is named more than 10 times, and in each of these 4 ranges one expert, the same for all blocks, is named exactly 10 times in every block.
All inputs are finite; a program needn't handle non-finite values.
Results may differ from a plain program's by a relative error of at most 0.015.
Values may be sent and summed in bfloat16 or wider, within the bound.
A program may use at most 128 MiB of HBM per device.

v0:
```python
import math
import jax
import jax.numpy as jnp
from jax import lax
from jax.sharding import PartitionSpec as P

HS = 64
NORM_EPS = 1e-06


def silu_parts(pre_gate):
    sigmoid = 1.0 / (1.0 + jnp.exp(-pre_gate))
    return (pre_gate * sigmoid, sigmoid * (1.0 + pre_gate * (1.0 - sigmoid)))


def expert_pass(arrived_rows, arrived_cot, expert_weights):
    pre_pair = jnp.einsum(
        "jmd,djcf->jmcf", arrived_rows, expert_weights[:, :, :2], preferred_element_type=jnp.float32
    )
    activated, act_slope = silu_parts(pre_pair[:, :, 0])
    up_value = pre_pair[:, :, 1]
    hidden = (activated * up_value).astype(jnp.bfloat16)
    expert_outs = jnp.einsum(
        "jmf,djf->jmd", hidden, expert_weights[:, :, 2], preferred_element_type=jnp.float32
    ).astype(jnp.bfloat16)
    back_hidden = jnp.einsum(
        "jmd,djf->jmf", arrived_cot, expert_weights[:, :, 2], preferred_element_type=jnp.float32
    )
    hidden_grads = jnp.stack(
        [back_hidden * up_value * act_slope, back_hidden * activated], axis=2
    ).astype(jnp.bfloat16)
    expert_grads = jnp.einsum(
        "jmcf,djcf->jmd", hidden_grads, expert_weights[:, :, :2], preferred_element_type=jnp.float32
    ).astype(jnp.bfloat16)
    return (expert_outs, expert_grads)


def per_device(
    stream,
    queries,
    keys,
    values,
    out_proj,
    norm_gain,
    expert_weights,
    expert_ids,
    gate_weights,
    out_cotangent,
):
    row_count, feature_width = stream.shape
    groups = lax.axis_size("rcv")
    local_count = expert_weights.shape[1]
    experts = local_count * groups
    top_count = expert_ids.shape[1]
    capacity = (5 * row_count * top_count + 4 * experts - 1) // (4 * experts)
    score_scale = 1.0 / math.sqrt(HS)
    flat_ids = expert_ids.reshape(-1)
    onehot = (flat_ids[:, None] == jnp.arange(experts, dtype=jnp.int32)[None, :]).astype(jnp.int32)
    slot_index = jnp.sum((jnp.cumsum(onehot, axis=0) - onehot) * onehot, axis=1)
    owner_rank = flat_ids // local_count
    local_expert = flat_ids % local_count
    cell_index = (local_expert * groups + owner_rank) * capacity + slot_index
    cell_total = experts * capacity
    token_index = jnp.arange(row_count * top_count, dtype=jnp.int32) // top_count
    source = jnp.full((cell_total,), row_count, jnp.int32).at[cell_index].set(token_index)

    def pack_rows(row_data):
        padded = jnp.concatenate([row_data, jnp.zeros((1, feature_width), row_data.dtype)], axis=0)
        return jnp.take(padded, source, axis=0).reshape(
            local_count, groups, capacity, feature_width
        )

    query_all, key_all, value_all = (
        lax.all_to_all(queries, "hd", split_axis=1, concat_axis=0, tiled=True),
        lax.all_to_all(keys, "hd", split_axis=1, concat_axis=0, tiled=True),
        lax.all_to_all(values, "hd", split_axis=1, concat_axis=0, tiled=True),
    )
    length = query_all.shape[0]
    head_count = query_all.shape[1] // HS
    block_rows = math.gcd(length, 512)
    key_heads = key_all.reshape(length, head_count, HS)
    value_heads = value_all.reshape(length, head_count, HS)

    def one_block(row_start):
        query_block = lax.dynamic_slice_in_dim(query_all, row_start, block_rows, 0).reshape(
            block_rows, head_count, HS
        )
        scores = (
            jnp.einsum("qhd,khd->hqk", query_block, key_heads, preferred_element_type=jnp.float32)
            * score_scale
        )
        row_max = jnp.max(scores, axis=2, keepdims=True)
        raw_weights = jnp.exp(scores - row_max)
        row_total = jnp.sum(raw_weights, axis=2)
        mixed_heads = jnp.einsum(
            "hqk,khd->qhd",
            raw_weights.astype(jnp.bfloat16),
            value_heads,
            preferred_element_type=jnp.float32,
        )
        result = mixed_heads / jnp.transpose(row_total)[:, :, None]
        return result.astype(jnp.bfloat16).reshape(block_rows, head_count * HS)

    starts = jnp.arange(length // block_rows, dtype=jnp.int32) * block_rows
    head_result = lax.map(one_block, starts).reshape(length, head_count * HS)
    attended = lax.all_to_all(head_result, "hd", split_axis=0, concat_axis=1, tiled=True)
    projected = jnp.dot(attended, out_proj, preferred_element_type=jnp.float32)
    mix_stream = (stream.astype(jnp.float32) + projected).astype(jnp.bfloat16)
    stream_wide = mix_stream.astype(jnp.float32)
    inverse = lax.rsqrt(jnp.mean(stream_wide * stream_wide, axis=1, keepdims=True) + NORM_EPS)
    normed = (norm_gain * stream_wide * inverse).astype(jnp.bfloat16)
    arrived_rows, arrived_cot = (
        lax.all_to_all(pack_rows(normed), "rcv", split_axis=1, concat_axis=1, tiled=True),
        lax.all_to_all(pack_rows(out_cotangent), "rcv", split_axis=1, concat_axis=1, tiled=True),
    )
    expert_outs, expert_grads = expert_pass(
        arrived_rows.reshape(local_count, groups * capacity, feature_width),
        arrived_cot.reshape(local_count, groups * capacity, feature_width),
        expert_weights,
    )
    back_out, back_grad = (
        lax.all_to_all(
            expert_outs.reshape(local_count, groups, capacity, feature_width),
            "rcv",
            split_axis=1,
            concat_axis=1,
            tiled=True,
        ),
        lax.all_to_all(
            expert_grads.reshape(local_count, groups, capacity, feature_width),
            "rcv",
            split_axis=1,
            concat_axis=1,
            tiled=True,
        ),
    )
    picked_out = jnp.take(back_out.reshape(cell_total, feature_width), cell_index, axis=0).reshape(
        row_count, top_count, feature_width
    )
    picked_grad = jnp.take(
        back_grad.reshape(cell_total, feature_width), cell_index, axis=0
    ).reshape(row_count, top_count, feature_width)
    gate_column = gate_weights[:, :, None]
    block_out = (
        stream_wide + jnp.sum(gate_column * picked_out.astype(jnp.float32), axis=1)
    ).astype(jnp.bfloat16)
    normed_grad = jnp.sum(gate_column * picked_grad.astype(jnp.float32), axis=1)
    weighted = norm_gain * normed_grad
    scaled = stream_wide * inverse
    stream_grad = out_cotangent.astype(jnp.float32) + inverse * (
        weighted - scaled * jnp.mean(weighted * scaled, axis=1, keepdims=True)
    )
    return (block_out, stream_grad.astype(jnp.bfloat16))


def solution(mesh):
    placed = (
        P(("rcv", "hd"), None),
        P(("rcv", "hd"), None),
        P(("rcv", "hd"), None),
        P(("rcv", "hd"), None),
        P(),
        P(),
        P(None, "rcv", None, None),
        P(("rcv", "hd"), None),
        P(("rcv", "hd"), None),
        P(("rcv", "hd"), None),
    )
    return jax.shard_map(
        per_device,
        mesh=mesh,
        in_specs=placed,
        out_specs=(P(("rcv", "hd"), None), P(("rcv", "hd"), None)),
        check_vma=False,
    )
```

profile of v0, /device:TPU:16, one launch (start us, length us, event | category | flops | bytes accessed | tf_op | source)
XLA Modules:
  0.0 263.5 jit_solution(5864382768889885304)
XLA Ops:
  2.6 4.4 %all-to-all-start.1 = ((bf16[128,8,128]{0,2,1:T(8,128)(2,1)}), bf16[128,8,128]{0,2,1:T(8,128)(2,1)S(1)}, u32[]{:S(2)}, u32[]{:S(2)}) async-start(bf16[128,8,128]{0,2,1:T(8,128)(2,1)} %bitcast.8), calls=%async_computation.1 | async-start | bytes 524288 | tf_op jit(solution)/shard_map/all_to_all | solution.py:75
  10.5 4.0 %all-to-all-done.1 = bf16[128,8,128]{0,2,1:T(8,128)(2,1)S(1)} async-done(((bf16[128,8,128]{0,2,1:T(8,128)(2,1)}), bf16[128,8,128]{0,2,1:T(8,128)(2,1)S(1)}, u32[]{:S(2)}, u32[]{:S(2)}) %all-to-all-start.1) | async-done | bytes 262176 | tf_op jit(solution)/shard_map/all_to_all | solution.py:75
  14.5 3.4 %all-to-all-start.2 = ((bf16[128,8,128]{0,2,1:T(8,128)(2,1)}), bf16[128,8,128]{0,2,1:T(8,128)(2,1)S(1)}, u32[]{:S(2)}, u32[]{:S(2)}) async-start(bf16[128,8,128]{0,2,1:T(8,128)(2,1)} %bitcast.10), calls=%async_computation.2 | async-start | bytes 524288 | tf_op jit(solution)/shard_map/all_to_all | solution.py:76
  19.0 6.4 %all-to-all-done.2 = bf16[128,8,128]{0,2,1:T(8,128)(2,1)S(1)} async-done(((bf16[128,8,128]{0,2,1:T(8,128)(2,1)}), bf16[128,8,128]{0,2,1:T(8,128)(2,1)S(1)}, u32[]{:S(2)}, u32[]{:S(2)}) %all-to-all-start.2) | async-done | bytes 262176 | tf_op jit(solution)/shard_map/all_to_all | solution.py:76
  25.4 3.4 %all-to-all-start = ((bf16[128,8,128]{0,2,1:T(8,128)(2,1)}), bf16[128,8,128]{0,2,1:T(8,128)(2,1)S(1)}, u32[]{:S(2)}, u32[]{:S(2)}) async-start(bf16[128,8,128]{0,2,1:T(8,128)(2,1)} %bitcast.5), calls=%async_computation | async-start | bytes 524288 | tf_op jit(solution)/shard_map/all_to_all | solution.py:74
  32.6 3.6 %all-to-all-done = bf16[128,8,128]{0,2,1:T(8,128)(2,1)S(1)} async-done(((bf16[128,8,128]{0,2,1:T(8,128)(2,1)}), bf16[128,8,128]{0,2,1:T(8,128)(2,1)S(1)}, u32[]{:S(2)}, u32[]{:S(2)}) %all-to-all-start) | async-done | bytes 262176 | tf_op jit(solution)/shard_map/all_to_all | solution.py:74
  36.4 12.4 %while.10 = (s32[]{:T(128)}, bf16[2,512,128]{2,1,0:T(8,128)(2,1)}, s32[2]{0:T(128)S(1)}, bf16[1024,128]{1,0:T(8,128)(2,1)S(1)}, bf16[1024,2,64]{0,2,1:T(8,128)(2...) while((s32[]{:T(128)}, bf16[2,512,128]{2,1,0:T(8,128)(2,1)}, ...), condition=%wide.region_3.4_spmd, body=%wide.region_0.3_spmd.sunk | while | flops 276953088 | bytes 15487659 | solution.py:105
  48.9 3.4 %all-to-all-start.3 = ((bf16[8,128,128]{2,1,0:T(8,128)(2,1)}), bf16[8,128,128]{2,1,0:T(8,128)(2,1)S(1)}, u32[]{:S(2)}, u32[]{:S(2)}) async-start(bf16[8,128,128]{2,1,0:T(8,128)(2,1)} %bitcast.118), calls=%async_computation.3 | async-start | bytes 524288 | tf_op jit(solution)/shard_map/all_to_all | solution.py:106
  52.4 3.5 %gather_fusion.2 = bf16[640,1024]{1,0:T(8,128)(2,1)} fusion(bf16[129,1024]{1,0:T(8,128)(2,1)S(1)} %concatenate.7, s32[1024]{0:T(1024)S(1)} %pad_clamp_fusion.1), kind=kCustom, calls=%fused_computation.2.clone | custom fusion | bytes 2624000 | tf_op jit(solution)/shard_map/jit(_take)/gather | solution.py:69
  55.9 3.9 %all-to-all-done.3 = bf16[8,128,128]{2,1,0:T(8,128)(2,1)S(1)} async-done(((bf16[8,128,128]{2,1,0:T(8,128)(2,1)}), bf16[8,128,128]{2,1,0:T(8,128)(2,1)S(1)}, u32[]{:S(2)}, u32[]{:S(2)}) %all-to-all-start.3) | async-done | bytes 262176 | tf_op jit(solution)/shard_map/all_to_all | solution.py:106
  61.5 3.5 %gather_fusion = bf16[640,1024]{1,0:T(8,128)(2,1)} fusion(bf16[129,1024]{1,0:T(8,128)(2,1)S(1)} %concatenate.6, s32[1024]{0:T(1024)S(1)} %pad_clamp_fusion.1), kind=kCustom, calls=%fused_computation.clone | custom fusion | bytes 2624000 | tf_op jit(solution)/shard_map/jit(_take)/gather | solution.py:69
  72.5 11.6 %all-to-all-start.4 = ((bf16[2,32,10,1024]{3,0,2,1:T(2,128)(2,1)}), bf16[2,32,10,1024]{3,0,2,1:T(2,128)(2,1)}, u32[]{:S(2)}, u32[]{:S(2)}) async-start(bf16[2,32,10,1024]{3,0,2,1:T(2,128)(2,1)} %copy.78), calls=%async_computation.4 | async-start | bytes 2621440 | tf_op jit(solution)/shard_map/all_to_all | solution.py:113
  87.0 30.5 %all-to-all-done.4 = bf16[2,32,10,1024]{3,0,2,1:T(2,128)(2,1)} async-done(((bf16[2,32,10,1024]{3,0,2,1:T(2,128)(2,1)}), bf16[2,32,10,1024]{3,0,2,1:T(2,128)(2,1)}, u32[]{:S(2)}, u32[]{:S(2)}) %all-to-all-start.4) | async-done | bytes 1310752 | tf_op jit(solution)/shard_map/all_to_all | solution.py:113
  117.5 5.6 %all-to-all-start.6 = ((bf16[2,32,10,1024]{3,0,2,1:T(2,128)(2,1)}), bf16[2,32,10,1024]{3,0,2,1:T(2,128)(2,1)}, u32[]{:S(2)}, u32[]{:S(2)}) async-start(bf16[2,32,10,1024]{3,0,2,1:T(2,128)(2,1)} %copy.85), calls=%async_computation.6 | async-start | bytes 2621440 | tf_op jit(solution)/shard_map/all_to_all | solution.py:114
  123.1 5.1 %slice.22 = bf16[1024,2,2,512]{3,1,2,0:T(2,128)(2,1)S(1)} slice(bf16[1024,2,3,512]{3,1,2,0:T(2,128)(2,1)} %param.22), slice={[0:1024], [0:2], [0:2], [0:512]} | slice | bytes 8388608 | tf_op jit(solution)/shard_map/slice | solution.py:18
  128.2 4.5 %slice.25 = bf16[1024,2,1,512]{3,1,2,0:T(2,128)(2,1)S(1)} slice(bf16[1024,2,3,512]{3,1,2,0:T(2,128)(2,1)} %param.22), slice={[0:1024], [0:2], [2:3], [0:512]} | slice | bytes 4194304 | tf_op jit(solution)/shard_map/slice | solution.py:24
  132.8 5.6 %fusion.16 = f32[2,320,2,512]{3,1,2,0:T(8,128)} fusion(bf16[1024,2,2,512]{3,1,2,0:T(2,128)(2,1)S(1)} %slice.22, bf16[2,320,1024,1]{2,0,1,3:T(2,128)(2,1)} %bitcast.19), kind=kOutput, calls=%fused_computation.18 | convolution fusion | flops 1342177280 | bytes 8126464 | tf_op jit(solution)/shard_map/jmd,djcf->jmcf/dot_general | solution.py:17
  138.3 17.2 %all-to-all-done.6 = bf16[2,32,10,1024]{3,0,2,1:T(2,128)(2,1)} async-done(((bf16[2,32,10,1024]{3,0,2,1:T(2,128)(2,1)}), bf16[2,32,10,1024]{3,0,2,1:T(2,128)(2,1)}, u32[]{:S(2)}, u32[]{:S(2)}) %all-to-all-start.6) | async-done | bytes 1310752 | tf_op jit(solution)/shard_map/all_to_all | solution.py:114
  155.6 3.6 %fusion.32 = (bf16[2,320,1,512]{3,1,0,2:T(8,128)(2,1)S(1)}, bf16[2,320,1,512]{3,1,0,2:T(8,128)(2,1)S(1)}) fusion(f32[2,320,2,512]{3,1,2,0:T(8,128)} %fusion.16, bf16[1024,2,1,512]{3,1,2,0:T(2,128)(2,1)S(1)} %slice.25, bf16[2,320,1024]{2,0,1:T(2,128)(2,1)} %bitcast.24), kind=kOutput, calls=%fused_computation.47 | convolution fusion | flops 675348480 | bytes 7340032 | tf_op jit(solution)/shard_map/jmd,djf->jmf/dot_general | solution.py:26
  163.3 5.6 %all-to-all-start.7 = ((bf16[2,32,10,1024]{3,0,2,1:T(2,128)(2,1)}), bf16[2,32,10,1024]{3,0,2,1:T(2,128)(2,1)S(1)}, u32[]{:S(2)}, u32[]{:S(2)}) async-start(bf16[2,32,10,1024]{3,0,2,1:T(2,128)(2,1)} %bitcast.28), calls=%async_computation.7 | async-start | bytes 2621440 | tf_op jit(solution)/shard_map/all_to_all | solution.py:129
  174.6 25.8 %all-to-all-done.7 = bf16[2,32,10,1024]{3,0,2,1:T(2,128)(2,1)S(1)} async-done(((bf16[2,32,10,1024]{3,0,2,1:T(2,128)(2,1)}), bf16[2,32,10,1024]{3,0,2,1:T(2,128)(2,1)S(1)}, u32[]{:S(2)}, u32[]{:S(2)}) %all-to-all-start.7) | async-done | bytes 1310752 | tf_op jit(solution)/shard_map/all_to_all | solution.py:129
  200.4 6.1 %all-to-all-start.5 = ((bf16[2,32,10,1024]{3,0,2,1:T(2,128)(2,1)}), bf16[2,32,10,1024]{3,0,2,1:T(2,128)(2,1)S(1)}, u32[]{:S(2)}, u32[]{:S(2)}) async-start(bf16[2,32,10,1024]{3,0,2,1:T(2,128)(2,1)} %bitcast.23), calls=%async_computation.5 | async-start | bytes 2621440 | tf_op jit(solution)/shard_map/all_to_all | solution.py:122
  211.1 27.4 %all-to-all-done.5 = bf16[2,32,10,1024]{3,0,2,1:T(2,128)(2,1)S(1)} async-done(((bf16[2,32,10,1024]{3,0,2,1:T(2,128)(2,1)}), bf16[2,32,10,1024]{3,0,2,1:T(2,128)(2,1)S(1)}, u32[]{:S(2)}, u32[]{:S(2)}) %all-to-all-start.5) | async-done | bytes 1310752 | tf_op jit(solution)/shard_map/all_to_all | solution.py:122
  256.2 5.5 %multiply_reduce_fusion.1 = (f32[128,1024]{1,0:T(8,128)S(1)}, f32[128,1024]{1,0:T(8,128)S(1)}) fusion(f32[128,4,1024]{2,1,0:T(4,128)} %reshape.240, f32[128,4]{1,0:T(8,128)S(1)} %copy.73, f32[128,4,1024]{2,1,0:T(4,128)} %reshape.239), kind=kLoop, calls=%fused_computation.22 | loop fusion | flops 1835008 | bytes 5244928 | tf_op jit(solution)/shard_map/reduce_sum | solution.py:147
  (106 shorter events, 64.8 us)
Async XLA Ops:
  0.6 59.3 %copy-start = (bf16[1024,1024]{1,0:T(8,128)(2,1)S(1)}, bf16[1024,1024]{1,0:T(8,128)(2,1)}, u32[]{:S(2)}) copy-start(bf16[1024,1024]{1,0:T(8,128)(2,1)} %param.20) | copy-start | bytes 6291460
  0.6 8.9 %copy-start.10 = (bf16[128,1024]{1,0:T(8,128)(2,1)S(1)}, bf16[128,1024]{1,0:T(8,128)(2,1)}, u32[]{:S(2)}) copy-start(bf16[128,1024]{1,0:T(8,128)(2,1)} %param.19) | copy-start | bytes 786436
  2.6 15.5 %copy-start.11 = (bf16[128,1024]{1,0:T(8,128)(2,1)S(1)}, bf16[128,1024]{1,0:T(8,128)(2,1)}, u32[]{:S(2)}) copy-start(bf16[128,1024]{1,0:T(8,128)(2,1)} %param.17) | copy-start | bytes 786436
  2.6 11.9 %all-to-all-start.1 = ((bf16[128,8,128]{0,2,1:T(8,128)(2,1)}), bf16[128,8,128]{0,2,1:T(8,128)(2,1)S(1)}, u32[]{:S(2)}, u32[]{:S(2)}) async-start(bf16[128,8,128]{0,2,1:T(8,128)(2,1)} %bitcast.8), calls=%async_computation.1 | async-start | bytes 524288 | tf_op jit(solution)/shard_map/all_to_all | solution.py:75
  14.5 10.8 %all-to-all-start.2 = ((bf16[128,8,128]{0,2,1:T(8,128)(2,1)}), bf16[128,8,128]{0,2,1:T(8,128)(2,1)S(1)}, u32[]{:S(2)}, u32[]{:S(2)}) async-start(bf16[128,8,128]{0,2,1:T(8,128)(2,1)} %bitcast.10), calls=%async_computation.2 | async-start | bytes 524288 | tf_op jit(solution)/shard_map/all_to_all | solution.py:76
  25.4 10.9 %all-to-all-start = ((bf16[128,8,128]{0,2,1:T(8,128)(2,1)}), bf16[128,8,128]{0,2,1:T(8,128)(2,1)S(1)}, u32[]{:S(2)}, u32[]{:S(2)}) async-start(bf16[128,8,128]{0,2,1:T(8,128)(2,1)} %bitcast.5), calls=%async_computation | async-start | bytes 524288 | tf_op jit(solution)/shard_map/all_to_all | solution.py:74
  36.4 15.9 %copy-start.8 = (bf16[128,1024]{1,0:T(8,128)(2,1)S(1)}, bf16[128,1024]{1,0:T(8,128)(2,1)}, u32[]{:S(2)}) copy-start(bf16[128,1024]{1,0:T(8,128)(2,1)} %param.25) | copy-start | bytes 786436
  40.0 1.0 copy-start.12
  46.2 1.0 copy-start.12
  48.9 10.9 %all-to-all-start.3 = ((bf16[8,128,128]{2,1,0:T(8,128)(2,1)}), bf16[8,128,128]{2,1,0:T(8,128)(2,1)S(1)}, u32[]{:S(2)}, u32[]{:S(2)}) async-start(bf16[8,128,128]{2,1,0:T(8,128)(2,1)} %bitcast.118), calls=%async_computation.3 | async-start | bytes 524288 | tf_op jit(solution)/shard_map/all_to_all | solution.py:106
  52.4 7.6 %copy-start.13 = (bf16[128,1024]{1,0:T(8,128)(2,1)S(1)}, bf16[128,1024]{1,0:T(8,128)(2,1)}, u32[]{:S(2)}) copy-start(bf16[128,1024]{1,0:T(8,128)(2,1)} %param.16) | copy-start | bytes 786436
  59.9 1.4 copy-start.14
  61.5 3.5 %copy-start.4 = (bf16[640,1024]{1,0:T(8,128)(2,1)S(1)}, bf16[640,1024]{1,0:T(8,128)(2,1)}, u32[]{:S(2)}) copy-start(bf16[640,1024]{1,0:T(8,128)(2,1)} %gather_fusion.2) | copy-start | bytes 3932164
  72.5 45.0 %all-to-all-start.4 = ((bf16[2,32,10,1024]{3,0,2,1:T(2,128)(2,1)}), bf16[2,32,10,1024]{3,0,2,1:T(2,128)(2,1)}, u32[]{:S(2)}, u32[]{:S(2)}) async-start(bf16[2,32,10,1024]{3,0,2,1:T(2,128)(2,1)} %copy.78), calls=%async_computation.4 | async-start | bytes 2621440 | tf_op jit(solution)/shard_map/all_to_all | solution.py:113
  117.5 38.1 %all-to-all-start.6 = ((bf16[2,32,10,1024]{3,0,2,1:T(2,128)(2,1)}), bf16[2,32,10,1024]{3,0,2,1:T(2,128)(2,1)}, u32[]{:S(2)}, u32[]{:S(2)}) async-start(bf16[2,32,10,1024]{3,0,2,1:T(2,128)(2,1)} %copy.85), calls=%async_computation.6 | async-start | bytes 2621440 | tf_op jit(solution)/shard_map/all_to_all | solution.py:114
  128.2 4.6 %copy-start.5 = (bf16[1024,2,2,512]{3,1,2,0:T(2,128)(2,1)}, bf16[1024,2,2,512]{3,1,2,0:T(2,128)(2,1)S(1)}, u32[]{:S(2)}) copy-start(bf16[1024,2,2,512]{3,1,2,0:T(2,128)(2,1)S(1)} %slice.22) | copy-start | bytes 12582916
  132.8 22.8 %copy-start.7 = (bf16[1024,2,1,512]{3,1,2,0:T(2,128)(2,1)}, bf16[1024,2,1,512]{3,1,2,0:T(2,128)(2,1)S(1)}, u32[]{:S(2)}) copy-start(bf16[1024,2,1,512]{3,1,2,0:T(2,128)(2,1)S(1)} %slice.25) | copy-start | bytes 6291460
  155.6 3.6 %copy-start.6 = (bf16[1024,2,2,512]{3,1,2,0:T(2,128)(2,1)S(1)}, bf16[1024,2,2,512]{3,1,2,0:T(2,128)(2,1)}, u32[]{:S(2)}) copy-start(bf16[1024,2,2,512]{3,1,2,0:T(2,128)(2,1)} %copy-done.5) | copy-start | bytes 12582916
  163.3 37.1 %all-to-all-start.7 = ((bf16[2,32,10,1024]{3,0,2,1:T(2,128)(2,1)}), bf16[2,32,10,1024]{3,0,2,1:T(2,128)(2,1)S(1)}, u32[]{:S(2)}, u32[]{:S(2)}) async-start(bf16[2,32,10,1024]{3,0,2,1:T(2,128)(2,1)} %bitcast.28), calls=%async_computation.7 | async-start | bytes 2621440 | tf_op jit(solution)/shard_map/all_to_all | solution.py:129
  200.4 6.1 %copy-start.15 = (f32[128,4]{0,1:T(4,128)S(1)}, f32[128,4]{0,1:T(4,128)}, u32[]{:S(2)}) copy-start(f32[128,4]{0,1:T(4,128)} %param.24) | copy-start | bytes 6148
  200.4 38.1 %all-to-all-start.5 = ((bf16[2,32,10,1024]{3,0,2,1:T(2,128)(2,1)}), bf16[2,32,10,1024]{3,0,2,1:T(2,128)(2,1)S(1)}, u32[]{:S(2)}, u32[]{:S(2)}) async-start(bf16[2,32,10,1024]{3,0,2,1:T(2,128)(2,1)} %bitcast.23), calls=%async_computation.5 | async-start | bytes 2621440 | tf_op jit(solution)/shard_map/all_to_all | solution.py:122
  256.2 5.5 %copy-start.3 = (f32[128,1024]{1,0:T(8,128)S(1)}, f32[128,1024]{1,0:T(8,128)}, u32[]{:S(2)}) copy-start(f32[128,1024]{1,0:T(8,128)} %copy-done.2) | copy-start | bytes 1572868
  256.2 5.7 %copy-start.9 = (bf16[128,1024]{1,0:T(8,128)(2,1)S(1)}, bf16[128,1024]{1,0:T(8,128)(2,1)}, u32[]{:S(2)}) copy-start(bf16[128,1024]{1,0:T(8,128)(2,1)} %param.25) | copy-start | bytes 786436
  261.7 1.8 copy-start.1
  (1 other events, 0.9 us)
where the time goes:
time: 265 us; the launch traced here: 264 us
  waiting for transfers between devices  119 us (45%)
  local copies, waits for them, and re-layouts  61.7 us (23%)
  starting transfers between devices  43.6 us (16%)
  matrix products  18.2 us (7%)
  other arithmetic  16 us (6%)
  loops' own time  3.97 us (1%)
    all_to_all x1, waiting for transfers between devices, per_device(): lax.all_to_all(pack_rows(normed), 'rcv', split_axis=1, concat_axis=1, til...  30.5 us
    all_to_all x1, waiting for transfers between devices, per_device(): lax.all_to_all(expert_outs.reshape(local_count, groups, capacity, feature...  27.4 us
    all_to_all x1, waiting for transfers between devices, per_device(): lax.all_to_all(expert_grads.reshape(local_count, groups, capacity, featur...  25.8 us
    all_to_all x1, waiting for transfers between devices, per_device(): lax.all_to_all(pack_rows(out_cotangent), 'rcv', split_axis=1, concat_axis...  17.2 us
    all_to_all x1, starting transfers between devices, per_device(): lax.all_to_all(pack_rows(normed), 'rcv', split_axis=1, concat_axis=1, til...  11.6 us
    reshape x4, local copies, waits for them, and re-layouts, pack_rows(): jnp.take(padded, source, axis=0)  7.68 us
    gather x2, local copies, waits for them, and re-layouts, pack_rows(): jnp.take(padded, source, axis=0)  6.95 us
    all_to_all x1, waiting for transfers between devices, per_device(): lax.all_to_all(values, 'hd', split_axis=1, concat_axis=0, tiled=True)  6.43 us
  transfers between devices with their start and end apart: 8, of which 8 were waited for; matrix products, arithmetic and copies ran while one was open for 15% of the time, Pallas kernels for 0%

commit v1 on v0

--- a/solution.py
+++ b/solution.py
@@ -110,7 +110,12 @@
     inverse = lax.rsqrt(jnp.mean(stream_wide * stream_wide, axis=1, keepdims=True) + NORM_EPS)
     normed = (norm_gain * stream_wide * inverse).astype(jnp.bfloat16)
     arrived_rows, arrived_cot = (
-        lax.all_to_all(pack_rows(normed), "rcv", split_axis=1, concat_axis=1, tiled=True),
+        jnp.concatenate(
+            lax.all_to_all(
+                jnp.stack(jnp.split(pack_rows(normed), lax.axis_size("rcv"), axis=1)), "rcv", 0, 0
+            ),
+            axis=1,
+        ),
         lax.all_to_all(pack_rows(out_cotangent), "rcv", split_axis=1, concat_axis=1, tiled=True),
     )
     expert_outs, expert_grads = expert_pass(

time: 265 us -> 265 us (level)
    reshape x4 -> x3, local copies, waits for them, and re-layouts: 7.68 us -> 5.24 us  [pack_rows(): jnp.take(padded, source, axis=0)]
    unnamed x35 -> x64, local copies, waits for them, and re-layouts: 5.98 us -> 6.59 us
  transfers between devices with their start and end apart: 8 -> 8, of which waited for: 8 -> 8; matrix products, arithmetic and copies ran while one was open for 15% -> 16% of each run, Pallas kernels for 0% -> 0%
where the time goes in v1:
time: 265 us; the launch traced here: 263 us
  waiting for transfers between devices  118 us (45%)
  local copies, waits for them, and re-layouts  62.3 us (24%)
  starting transfers between devices  42.9 us (16%)
  matrix products  18.2 us (7%)
  other arithmetic  16.1 us (6%)
  loops' own time  3.97 us (1%)
    all_to_all x1, waiting for transfers between devices, per_device(): lax.all_to_all(jnp.stack(jnp.split(pack_rows(normed), lax.axis_size('rcv'...  30.5 us
    all_to_all x1, waiting for transfers between devices, per_device(): lax.all_to_all(expert_outs.reshape(local_count, groups, capacity, feature...  27.4 us
    all_to_all x1, waiting for transfers between devices, per_device(): lax.all_to_all(expert_grads.reshape(local_count, groups, capacity, featur...  26.2 us
    all_to_all x1, waiting for transfers between devices, per_device(): lax.all_to_all(pack_rows(out_cotangent), 'rcv', split_axis=1, concat_axis...  17.2 us
    all_to_all x1, starting transfers between devices, per_device(): lax.all_to_all(jnp.stack(jnp.split(pack_rows(normed), lax.axis_size('rcv'...  11.6 us
    gather x2, local copies, waits for them, and re-layouts, pack_rows(): jnp.take(padded, source, axis=0)  6.95 us
    unnamed x64, local copies, waits for them, and re-layouts  6.59 us
    all_to_all x1, waiting for transfers between devices, per_device(): lax.all_to_all(values, 'hd', split_axis=1, concat_axis=0, tiled=True)  6.43 us
  transfers between devices with their start and end apart: 8, of which 8 were waited for; matrix products, arithmetic and copies ran while one was open for 16% of the time, Pallas kernels for 0%

profile of v1, /device:TPU:16, one launch (start us, length us, event | category | flops | bytes accessed | tf_op | source)
XLA Modules:
  0.0 263.2 jit_solution(12703323422584909223)
XLA Ops:
  2.6 4.3 %all-to-all-start.1 = ((bf16[128,8,128]{0,2,1:T(8,128)(2,1)}), bf16[128,8,128]{0,2,1:T(8,128)(2,1)S(1)}, u32[]{:S(2)}, u32[]{:S(2)}) async-start(bf16[128,8,128]{0,2,1:T(8,128)(2,1)} %bitcast.8), calls=%async_computation.1 | async-start | bytes 524288 | tf_op jit(solution)/shard_map/all_to_all | solution.py:75
  14.4 3.4 %all-to-all-start.2 = ((bf16[128,8,128]{0,2,1:T(8,128)(2,1)}), bf16[128,8,128]{0,2,1:T(8,128)(2,1)S(1)}, u32[]{:S(2)}, u32[]{:S(2)}) async-start(bf16[128,8,128]{0,2,1:T(8,128)(2,1)} %bitcast.10), calls=%async_computation.2 | async-start | bytes 524288 | tf_op jit(solution)/shard_map/all_to_all | solution.py:76
  18.8 6.4 %all-to-all-done.2 = bf16[128,8,128]{0,2,1:T(8,128)(2,1)S(1)} async-done(((bf16[128,8,128]{0,2,1:T(8,128)(2,1)}), bf16[128,8,128]{0,2,1:T(8,128)(2,1)S(1)}, u32[]{:S(2)}, u32[]{:S(2)}) %all-to-all-start.2) | async-done | bytes 262176 | tf_op jit(solution)/shard_map/all_to_all | solution.py:76
  25.3 3.4 %all-to-all-start = ((bf16[128,8,128]{0,2,1:T(8,128)(2,1)}), bf16[128,8,128]{0,2,1:T(8,128)(2,1)S(1)}, u32[]{:S(2)}, u32[]{:S(2)}) async-start(bf16[128,8,128]{0,2,1:T(8,128)(2,1)} %bitcast.5), calls=%async_computation | async-start | bytes 524288 | tf_op jit(solution)/shard_map/all_to_all | solution.py:74
  32.5 3.7 %all-to-all-done = bf16[128,8,128]{0,2,1:T(8,128)(2,1)S(1)} async-done(((bf16[128,8,128]{0,2,1:T(8,128)(2,1)}), bf16[128,8,128]{0,2,1:T(8,128)(2,1)S(1)}, u32[]{:S(2)}, u32[]{:S(2)}) %all-to-all-start) | async-done | bytes 262176 | tf_op jit(solution)/shard_map/all_to_all | solution.py:74
  36.3 12.5 %while.10 = (s32[]{:T(128)}, bf16[2,512,128]{2,1,0:T(8,128)(2,1)}, s32[2]{0:T(128)S(1)}, bf16[1024,128]{1,0:T(8,128)(2,1)S(1)}, bf16[1024,2,64]{0,2,1:T(8,128)(2...) while((s32[]{:T(128)}, bf16[2,512,128]{2,1,0:T(8,128)(2,1)}, ...), condition=%wide.region_3.4_spmd, body=%wide.region_0.3_spmd.sunk | while | flops 276953088 | bytes 15487659 | solution.py:105
  48.8 3.4 %all-to-all-start.3 = ((bf16[8,128,128]{2,1,0:T(8,128)(2,1)}), bf16[8,128,128]{2,1,0:T(8,128)(2,1)S(1)}, u32[]{:S(2)}, u32[]{:S(2)}) async-start(bf16[8,128,128]{2,1,0:T(8,128)(2,1)} %bitcast.310), calls=%async_computation.3 | async-start | bytes 524288 | tf_op jit(solution)/shard_map/all_to_all | solution.py:106
  52.2 3.5 %gather_fusion.2 = bf16[640,1024]{1,0:T(8,128)(2,1)} fusion(bf16[129,1024]{1,0:T(8,128)(2,1)S(1)} %concatenate.7, s32[1024]{0:T(1024)S(1)} %pad_clamp_fusion.1), kind=kCustom, calls=%fused_computation.2.clone | custom fusion | bytes 2624000 | tf_op jit(solution)/shard_map/jit(_take)/gather | solution.py:69
  55.7 3.9 %all-to-all-done.3 = bf16[8,128,128]{2,1,0:T(8,128)(2,1)S(1)} async-done(((bf16[8,128,128]{2,1,0:T(8,128)(2,1)}), bf16[8,128,128]{2,1,0:T(8,128)(2,1)S(1)}, u32[]{:S(2)}, u32[]{:S(2)}) %all-to-all-start.3) | async-done | bytes 262176 | tf_op jit(solution)/shard_map/all_to_all | solution.py:106
  61.4 3.5 %gather_fusion = bf16[640,1024]{1,0:T(8,128)(2,1)} fusion(bf16[129,1024]{1,0:T(8,128)(2,1)S(1)} %concatenate.6, s32[1024]{0:T(1024)S(1)} %pad_clamp_fusion.1), kind=kCustom, calls=%fused_computation.clone | custom fusion | bytes 2624000 | tf_op jit(solution)/shard_map/jit(_take)/gather | solution.py:69
  72.8 11.6 %all-to-all-start.4 = ((bf16[32,2,1,10,1024]{4,1,3,2,0:T(2,128)(2,1)}), bf16[32,2,1,10,1024]{4,1,3,2,0:T(2,128)(2,1)}, u32[]{:S(2)}, u32[]{:S(2)}) async-start(bf16[32,2,1,10,1024]{4,1,3,2,0:T(2,128)(2,1)} %copy.203), calls=%async_computation.4 | async-start | bytes 2621440 | tf_op jit(solution)/shard_map/all_to_all | solution.py:114
  87.3 30.5 %all-to-all-done.4 = bf16[32,2,1,10,1024]{4,1,3,2,0:T(2,128)(2,1)} async-done(((bf16[32,2,1,10,1024]{4,1,3,2,0:T(2,128)(2,1)}), bf16[32,2,1,10,1024]{4,1,3,2,0:T(2,128)(2,1)}, u32[]{:S(2)}, u32[]{:S(2)}) %all-to-all-start.4) | async-done | bytes 1310752 | tf_op jit(solution)/shard_map/all_to_all | solution.py:114
  117.8 5.6 %all-to-all-start.6 = ((bf16[2,32,10,1024]{3,0,2,1:T(2,128)(2,1)}), bf16[2,32,10,1024]{3,0,2,1:T(2,128)(2,1)}, u32[]{:S(2)}, u32[]{:S(2)}) async-start(bf16[2,32,10,1024]{3,0,2,1:T(2,128)(2,1)} %copy.210), calls=%async_computation.6 | async-start | bytes 2621440 | tf_op jit(solution)/shard_map/all_to_all | solution.py:119
  123.4 5.1 %slice.22 = bf16[1024,2,2,512]{3,1,2,0:T(2,128)(2,1)S(1)} slice(bf16[1024,2,3,512]{3,1,2,0:T(2,128)(2,1)} %param.22), slice={[0:1024], [0:2], [0:2], [0:512]} | slice | bytes 8388608 | tf_op jit(solution)/shard_map/slice | solution.py:18
  128.5 4.5 %slice.25 = bf16[1024,2,1,512]{3,1,2,0:T(2,128)(2,1)S(1)} slice(bf16[1024,2,3,512]{3,1,2,0:T(2,128)(2,1)} %param.22), slice={[0:1024], [0:2], [2:3], [0:512]} | slice | bytes 4194304 | tf_op jit(solution)/shard_map/slice | solution.py:24
  133.1 5.6 %fusion.16 = f32[2,320,2,512]{3,1,2,0:T(8,128)} fusion(bf16[1024,2,2,512]{3,1,2,0:T(2,128)(2,1)S(1)} %slice.22, bf16[2,320,1024,1]{2,0,1,3:T(2,128)(2,1)} %bitcast.52), kind=kOutput, calls=%fused_computation.18 | convolution fusion | flops 1342177280 | bytes 8126464 | tf_op jit(solution)/shard_map/jmd,djcf->jmcf/dot_general | solution.py:17
  138.7 17.2 %all-to-all-done.6 = bf16[2,32,10,1024]{3,0,2,1:T(2,128)(2,1)} async-done(((bf16[2,32,10,1024]{3,0,2,1:T(2,128)(2,1)}), bf16[2,32,10,1024]{3,0,2,1:T(2,128)(2,1)}, u32[]{:S(2)}, u32[]{:S(2)}) %all-to-all-start.6) | async-done | bytes 1310752 | tf_op jit(solution)/shard_map/all_to_all | solution.py:119
  155.9 3.6 %fusion.32 = (bf16[2,320,1,512]{3,1,0,2:T(8,128)(2,1)S(1)}, bf16[2,320,1,512]{3,1,0,2:T(8,128)(2,1)S(1)}) fusion(f32[2,320,2,512]{3,1,2,0:T(8,128)} %fusion.16, bf16[1024,2,1,512]{3,1,2,0:T(2,128)(2,1)S(1)} %slice.25, bf16[2,320,1024]{2,0,1:T(2,128)(2,1)} %bitcast.57), kind=kOutput, calls=%fused_computation.47 | convolution fusion | flops 675348480 | bytes 7340032 | tf_op jit(solution)/shard_map/jmd,djf->jmf/dot_general | solution.py:26
  163.6 5.6 %all-to-all-start.7 = ((bf16[2,32,10,1024]{3,0,2,1:T(2,128)(2,1)}), bf16[2,32,10,1024]{3,0,2,1:T(2,128)(2,1)S(1)}, u32[]{:S(2)}, u32[]{:S(2)}) async-start(bf16[2,32,10,1024]{3,0,2,1:T(2,128)(2,1)} %bitcast.61), calls=%async_computation.7 | async-start | bytes 2621440 | tf_op jit(solution)/shard_map/all_to_all | solution.py:134
  169.2 3.3 %fusion.22 = bf16[2,320,1024]{2,1,0:T(8,128)(2,1)S(1)} fusion(bf16[1024,2,1,512]{3,1,2,0:T(2,128)(2,1)} %copy-done.7, f32[2,320,2,512]{3,1,2,0:T(8,128)} %fusion.16), kind=kOutput, calls=%fused_computation.26 | convolution fusion | flops 673710080 | bytes 6029312 | tf_op jit(solution)/shard_map/jmf,djf->jmd/dot_general | solution.py:23
  174.9 26.2 %all-to-all-done.7 = bf16[2,32,10,1024]{3,0,2,1:T(2,128)(2,1)S(1)} async-done(((bf16[2,32,10,1024]{3,0,2,1:T(2,128)(2,1)}), bf16[2,32,10,1024]{3,0,2,1:T(2,128)(2,1)S(1)}, u32[]{:S(2)}, u32[]{:S(2)}) %all-to-all-start.7) | async-done | bytes 1310752 | tf_op jit(solution)/shard_map/all_to_all | solution.py:134
  201.1 5.6 %all-to-all-start.5 = ((bf16[2,32,10,1024]{3,0,2,1:T(2,128)(2,1)}), bf16[2,32,10,1024]{3,0,2,1:T(2,128)(2,1)S(1)}, u32[]{:S(2)}, u32[]{:S(2)}) async-start(bf16[2,32,10,1024]{3,0,2,1:T(2,128)(2,1)} %bitcast.56), calls=%async_computation.5 | async-start | bytes 2621440 | tf_op jit(solution)/shard_map/all_to_all | solution.py:127
  211.3 27.4 %all-to-all-done.5 = bf16[2,32,10,1024]{3,0,2,1:T(2,128)(2,1)S(1)} async-done(((bf16[2,32,10,1024]{3,0,2,1:T(2,128)(2,1)}), bf16[2,32,10,1024]{3,0,2,1:T(2,128)(2,1)S(1)}, u32[]{:S(2)}, u32[]{:S(2)}) %all-to-all-start.5) | async-done | bytes 1310752 | tf_op jit(solution)/shard_map/all_to_all | solution.py:127
  256.4 5.6 %multiply_reduce_fusion.1 = (f32[128,1024]{1,0:T(8,128)S(1)}, f32[128,1024]{1,0:T(8,128)S(1)}) fusion(f32[128,4,1024]{2,1,0:T(4,128)} %reshape.240, f32[128,4]{1,0:T(8,128)S(1)} %copy.167, f32[128,4,1024]{2,1,0:T(4,128)} %reshape.239), kind=kLoop, calls=%fused_computation.22 | loop fusion | flops 1835008 | bytes 5244928 | tf_op jit(solution)/shard_map/reduce_sum | solution.py:152
  (136 shorter events, 65.2 us)
Async XLA Ops:
  0.6 59.2 %copy-start = (bf16[1024,1024]{1,0:T(8,128)(2,1)S(1)}, bf16[1024,1024]{1,0:T(8,128)(2,1)}, u32[]{:S(2)}) copy-start(bf16[1024,1024]{1,0:T(8,128)(2,1)} %param.20) | copy-start | bytes 6291460
  0.6 17.3 %copy-start.10 = (bf16[128,1024]{1,0:T(8,128)(2,1)S(1)}, bf16[128,1024]{1,0:T(8,128)(2,1)}, u32[]{:S(2)}) copy-start(bf16[128,1024]{1,0:T(8,128)(2,1)} %param.17) | copy-start | bytes 786436
  2.6 11.8 %all-to-all-start.1 = ((bf16[128,8,128]{0,2,1:T(8,128)(2,1)}), bf16[128,8,128]{0,2,1:T(8,128)(2,1)S(1)}, u32[]{:S(2)}, u32[]{:S(2)}) async-start(bf16[128,8,128]{0,2,1:T(8,128)(2,1)} %bitcast.8), calls=%async_computation.1 | async-start | bytes 524288 | tf_op jit(solution)/shard_map/all_to_all | solution.py:75
  14.4 10.8 %all-to-all-start.2 = ((bf16[128,8,128]{0,2,1:T(8,128)(2,1)}), bf16[128,8,128]{0,2,1:T(8,128)(2,1)S(1)}, u32[]{:S(2)}, u32[]{:S(2)}) async-start(bf16[128,8,128]{0,2,1:T(8,128)(2,1)} %bitcast.10), calls=%async_computation.2 | async-start | bytes 524288 | tf_op jit(solution)/shard_map/all_to_all | solution.py:76
  25.3 10.9 %all-to-all-start = ((bf16[128,8,128]{0,2,1:T(8,128)(2,1)}), bf16[128,8,128]{0,2,1:T(8,128)(2,1)S(1)}, u32[]{:S(2)}, u32[]{:S(2)}) async-start(bf16[128,8,128]{0,2,1:T(8,128)(2,1)} %bitcast.5), calls=%async_computation | async-start | bytes 524288 | tf_op jit(solution)/shard_map/all_to_all | solution.py:74
  36.3 15.9 %copy-start.8 = (bf16[128,1024]{1,0:T(8,128)(2,1)S(1)}, bf16[128,1024]{1,0:T(8,128)(2,1)}, u32[]{:S(2)}) copy-start(bf16[128,1024]{1,0:T(8,128)(2,1)} %param.25) | copy-start | bytes 786436
  39.9 1.0 copy-start.11
  46.1 1.0 copy-start.11
  48.8 10.9 %all-to-all-start.3 = ((bf16[8,128,128]{2,1,0:T(8,128)(2,1)}), bf16[8,128,128]{2,1,0:T(8,128)(2,1)S(1)}, u32[]{:S(2)}, u32[]{:S(2)}) async-start(bf16[8,128,128]{2,1,0:T(8,128)(2,1)} %bitcast.310), calls=%async_computation.3 | async-start | bytes 524288 | tf_op jit(solution)/shard_map/all_to_all | solution.py:106
  52.2 7.6 %copy-start.12 = (bf16[128,1024]{1,0:T(8,128)(2,1)S(1)}, bf16[128,1024]{1,0:T(8,128)(2,1)}, u32[]{:S(2)}) copy-start(bf16[128,1024]{1,0:T(8,128)(2,1)} %param.16) | copy-start | bytes 786436
  55.7 5.5 %copy-start.13 = (f32[1024]{0:T(1024)S(1)}, f32[1024]{0:T(1024)}, u32[]{:S(2)}) copy-start(f32[1024]{0:T(1024)} %param.21) | copy-start | bytes 12292
  60.4 0.8 copy-start.2
  61.4 3.5 %copy-start.4 = (bf16[640,1024]{1,0:T(8,128)(2,1)S(1)}, bf16[640,1024]{1,0:T(8,128)(2,1)}, u32[]{:S(2)}) copy-start(bf16[640,1024]{1,0:T(8,128)(2,1)} %gather_fusion.2) | copy-start | bytes 3932164
  72.8 45.0 %all-to-all-start.4 = ((bf16[32,2,1,10,1024]{4,1,3,2,0:T(2,128)(2,1)}), bf16[32,2,1,10,1024]{4,1,3,2,0:T(2,128)(2,1)}, u32[]{:S(2)}, u32[]{:S(2)}) async-start(bf16[32,2,1,10,1024]{4,1,3,2,0:T(2,128)(2,1)} %copy.203), calls=%async_computation.4 | async-start | bytes 2621440 | tf_op jit(solution)/shard_map/all_to_all | solution.py:114
  117.8 38.1 %all-to-all-start.6 = ((bf16[2,32,10,1024]{3,0,2,1:T(2,128)(2,1)}), bf16[2,32,10,1024]{3,0,2,1:T(2,128)(2,1)}, u32[]{:S(2)}, u32[]{:S(2)}) async-start(bf16[2,32,10,1024]{3,0,2,1:T(2,128)(2,1)} %copy.210), calls=%async_computation.6 | async-start | bytes 2621440 | tf_op jit(solution)/shard_map/all_to_all | solution.py:119
  128.5 4.6 %copy-start.5 = (bf16[1024,2,2,512]{3,1,2,0:T(2,128)(2,1)}, bf16[1024,2,2,512]{3,1,2,0:T(2,128)(2,1)S(1)}, u32[]{:S(2)}) copy-start(bf16[1024,2,2,512]{3,1,2,0:T(2,128)(2,1)S(1)} %slice.22) | copy-start | bytes 12582916
  133.1 22.8 %copy-start.7 = (bf16[1024,2,1,512]{3,1,2,0:T(2,128)(2,1)}, bf16[1024,2,1,512]{3,1,2,0:T(2,128)(2,1)S(1)}, u32[]{:S(2)}) copy-start(bf16[1024,2,1,512]{3,1,2,0:T(2,128)(2,1)S(1)} %slice.25) | copy-start | bytes 6291460
  155.9 3.6 %copy-start.6 = (bf16[1024,2,2,512]{3,1,2,0:T(2,128)(2,1)S(1)}, bf16[1024,2,2,512]{3,1,2,0:T(2,128)(2,1)}, u32[]{:S(2)}) copy-start(bf16[1024,2,2,512]{3,1,2,0:T(2,128)(2,1)} %copy-done.5) | copy-start | bytes 12582916
  163.6 37.5 %all-to-all-start.7 = ((bf16[2,32,10,1024]{3,0,2,1:T(2,128)(2,1)}), bf16[2,32,10,1024]{3,0,2,1:T(2,128)(2,1)S(1)}, u32[]{:S(2)}, u32[]{:S(2)}) async-start(bf16[2,32,10,1024]{3,0,2,1:T(2,128)(2,1)} %bitcast.61), calls=%async_computation.7 | async-start | bytes 2621440 | tf_op jit(solution)/shard_map/all_to_all | solution.py:134
  172.5 34.2 %copy-start.14 = (f32[128,4]{0,1:T(4,128)S(1)}, f32[128,4]{0,1:T(4,128)}, u32[]{:S(2)}) copy-start(f32[128,4]{0,1:T(4,128)} %param.24) | copy-start | bytes 6148
  201.1 37.6 %all-to-all-start.5 = ((bf16[2,32,10,1024]{3,0,2,1:T(2,128)(2,1)}), bf16[2,32,10,1024]{3,0,2,1:T(2,128)(2,1)S(1)}, u32[]{:S(2)}, u32[]{:S(2)}) async-start(bf16[2,32,10,1024]{3,0,2,1:T(2,128)(2,1)} %bitcast.56), calls=%async_computation.5 | async-start | bytes 2621440 | tf_op jit(solution)/shard_map/all_to_all | solution.py:127
  256.4 5.6 %copy-start.3 = (f32[128,1024]{1,0:T(8,128)S(1)}, f32[128,1024]{1,0:T(8,128)}, u32[]{:S(2)}) copy-start(f32[128,1024]{1,0:T(8,128)} %copy-done.2) | copy-start | bytes 1572868
  256.4 5.8 %copy-start.9 = (bf16[128,1024]{1,0:T(8,128)(2,1)S(1)}, bf16[128,1024]{1,0:T(8,128)(2,1)}, u32[]{:S(2)}) copy-start(bf16[128,1024]{1,0:T(8,128)(2,1)} %param.25) | copy-start | bytes 786436
  256.4 6.8 %copy-start.1 = (bf16[1024,1024]{1,0:T(8,128)(2,1)S(1)}, bf16[1024,1024]{1,0:T(8,128)(2,1)}, u32[]{:S(2)}) copy-start(bf16[1024,1024]{1,0:T(8,128)(2,1)} %param.20) | copy-start | bytes 6291460
